TPU v7x, 32 devices: a whole 2x2x4 slice. The times are simulated.
32 devices in a mesh: tm: 8 (over z, x), state: 4 (over y, core).
Axes of the slice: x: 2, y: 2, z: 4, core: 2. Of those that a mesh axis runs over, the one named last changes fastest.
Arguments:
- trans_weight: bfloat16 [8, 2048, 2048], P('tm', None, 'state'), may hold values from 6e-06 to 163000
- pattern: int32 [16, 16], replicated, may hold values 0 or 1
- boundary: int32 [8], P('tm'), may hold values 0 or 1
- log_emit: float32 [8, 2048], P('tm', 'state'), may hold values from -63 to 153
Outputs:
- quad_op: float32 [4096, 2048], P('tm', 'state')
All inputs are finite; a program needn't handle non-finite values. No bound on the sum of `boundary` on one device may be relied on, other than what follows from the above.
Results may differ from a plain program's by a relative error of at most 0.0003.
Values sent between devices are 32-bit elements; how exact they have to be, the bound alone decides.
A program may use at most 64 MiB of HBM per device.

v0:
```python
import jax
import jax.numpy as jnp
from jax import lax
from jax.sharding import PartitionSpec as P

BLOCK = 128


def from_partner(shard, axis, apart):
    return lax.ppermute(shard, axis, [(i, i ^ 1 << apart) for i in range(lax.axis_size(axis))])


def block_mask(pattern, row_count, col_start, col_count):
    block_count = pattern.shape[0]
    row_ids = jnp.arange(row_count, dtype=jnp.int32) // BLOCK
    col_ids = (col_start + jnp.arange(col_count, dtype=jnp.int32)) // BLOCK
    blocks = jnp.arange(block_count, dtype=jnp.int32)
    row_hot = (row_ids[:, None] == blocks[None, :]).astype(jnp.float32)
    col_hot = (blocks[:, None] == col_ids[None, :]).astype(jnp.float32)
    lookup = pattern.astype(jnp.float32)
    return jnp.dot(jnp.dot(row_hot, lookup), col_hot)


def combine(left_log, right_log):
    row_top = jnp.max(left_log, axis=1, keepdims=True)
    col_top = jnp.max(right_log, axis=0, keepdims=True)
    lead = jnp.exp(left_log - row_top).astype(jnp.bfloat16)
    trail = jnp.exp(right_log - col_top).astype(jnp.bfloat16)
    summed = jnp.dot(lead, trail, preferred_element_type=jnp.float32)
    return row_top + col_top + jnp.log(summed)


def on_device(trans_weight, pattern, boundary, log_emit):
    weight = trans_weight[0]
    states, col_width = weight.shape
    col_start = lax.axis_index("state") * col_width
    restart = 0.0001 + 0.4999 * boundary.astype(jnp.float32)
    mask_table = block_mask(pattern, states, col_start, col_width)
    mixture = (1.0 - restart) * (4.0 / states) * weight.astype(
        jnp.float32
    ) * mask_table + restart / states
    own_op = jnp.log(mixture) + log_emit
    tm_index = lax.axis_index("tm")
    half_index = tm_index % 2
    partner_op = from_partner(own_op, "tm", 0)
    first_op = jnp.where(half_index == 0, own_op, partner_op)
    second_op = jnp.where(half_index == 0, partner_op, own_op)
    row_start = half_index * (states // 2)
    row_count = states // 2
    left_slab = lax.dynamic_slice_in_dim(first_op, row_start, row_count, 0)
    left_full = lax.all_gather(left_slab, "state", axis=1, tiled=True)
    pair_op = combine(left_full, second_op)
    other_half = from_partner(pair_op, "tm", 0)
    own_pair = jnp.where(
        half_index == 0,
        jnp.concatenate([pair_op, other_half], axis=0),
        jnp.concatenate([other_half, pair_op], axis=0),
    )
    other_pair = from_partner(own_pair, "tm", 1)
    leading = tm_index // 2 % 2 == 0
    quarter = states // 4
    quarter_start = tm_index % 4 * quarter
    own_rows = lax.dynamic_slice_in_dim(own_pair, quarter_start, quarter, 0)
    other_rows = lax.dynamic_slice_in_dim(other_pair, quarter_start, quarter, 0)
    quad_slab = jnp.where(leading, own_rows, other_rows)
    right_pair = jnp.where(leading, other_pair, own_pair)
    quad_left = lax.all_gather(quad_slab, "state", axis=1, tiled=True)
    return combine(quad_left, right_pair)


def solution(mesh):
    return jax.shard_map(
        on_device,
        mesh=mesh,
        in_specs=(P("tm", None, "state"), P(), P("tm"), P("tm", "state")),
        out_specs=P("tm", "state"),
        check_vma=False,
    )
```

profile of v0, /device:TPU:0, one launch (start us, length us, event | category | flops | bytes accessed | tf_op | source)
XLA Modules:
  0.0 375.7 jit_solution(6337932703887638775)
XLA Ops:
  6.5 0.0 all-gather.3.cloned.1.call-start
  7.2 5.0 %fusion.3 = f32[2048,512]{1,0:T(8,128)} fusion(bf16[1,2048,512]{2,1,0:T(8,128)(2,1)} %param.4, f32[512]{0:T(512)} %bitcast.11, f32[]{:T(128)} %bitcast.2, f32[]{:T(128)} %bitcast, s32[2048]{0:T(1024)S(1)} %add_select_fusion, s32[512]{0:T(512)S(1)} %add_select_fusion.1, s32[16,16]{1,0:T(8,128)} %param.5), kind=kOutput, calls=%fused_computation.6 | convolution fusion | flops 39887104 | bytes 6304776 | tf_op jit(solution)/shard_map/dot_general | solution.py:21
  12.2 2.9 collective-permute-start
  15.1 90.9 %collective-permute-done = f32[2048,512]{1,0:T(8,128)} collective-permute-done((f32[2048,512]{1,0:T(8,128)}, f32[2048,512]{1,0:T(8,128)}, u32[]{:S(2)}, u32[]{:S(2)}) %collective-permute-start) | collective-permute-done | bytes 4194336 | tf_op jit(solution)/shard_map/ppermute | solution.py:10
  106.0 4.0 %dynamic-slice_select_fusion = f32[1024,512]{1,0:T(8,128)} fusion(f32[2048,512]{1,0:T(8,128)} %collective-permute-done, s32[]{:T(128)S(6)} %select_n.82, f32[2048,512]{1,0:T(8,128)} %fusion.3, pred[]{:T(512)S(6)} %eq.39), kind=kLoop, calls=%fused_computation.12 | loop fusion | flops 524288 | bytes 6291461 | tf_op jit(solution)/shard_map/jit(_where)/select_n | solution.py:46
  110.1 0.0 all-gather.3.cloned.1.call-update
  110.1 0.0 all-gather.5.cloned.1.call-start
  110.1 2.7 fusion.9
  112.8 57.2 %all-gather.3.cloned.1.call-done = f32[1024,2048]{1,0:T(8,128)} async-done(((f32[1024,512]{1,0:T(8,128)}), f32[1024,2048]{1,0:T(8,128)}) %all-gather.3.cloned.1.call-update) | async-done | bytes 8388624 | tf_op jit(solution)/shard_map/all_gather | solution.py:51
  170.0 3.8 %reduce_max.36 = f32[1024]{0:T(1024)S(1)} reduce(f32[1024,2048]{1,0:T(8,128)} %all-gather.3.cloned.1.call-done, f32[]{:T(128)} %constant.88.clone.1), dimensions={1}, to_apply=%region_0.1 | reduce | flops 2096128 | bytes 8392708 | tf_op jit(solution)/shard_map/reduce_max | solution.py:25
  173.9 6.5 %log_add_fusion = f32[1024,512]{1,0:T(8,128)S(1)} fusion(f32[512]{0:T(512)S(1)} %fusion.9, f32[2048,512]{1,0:T(8,128)} %collective-permute-done, f32[2048,512]{1,0:T(8,128)} %fusion.3, pred[]{:T(512)S(6)} %eq.39, f32[1024,2048]{1,0:T(8,128)} %all-gather.3.cloned.1.call-done, f32[1024]{0:T(1024)S(1)} %reduce_max.36), kind=kOutput, calls=%fused_computation.15 | convolution fusion | flops 2155872256 | bytes 18880512 | tf_op jit(solution)/shard_map/dot_general | solution.py:29
  180.3 1.5 collective-permute-start.1
  181.9 46.3 %collective-permute-done.1 = f32[1024,512]{1,0:T(8,128)S(1)} collective-permute-done((f32[1024,512]{1,0:T(8,128)S(1)}, f32[1024,512]{1,0:T(8,128)S(1)}, u32[]{:S(2)}, u32[]{:S(2)}) %collective-permute-start.1) | collective-permute-done | bytes 2097184 | tf_op jit(solution)/shard_map/ppermute | solution.py:10
  228.2 2.8 maximum_select_fusion
  231.0 1.5 collective-permute-start.2
  232.5 90.8 %collective-permute-done.2 = f32[2048,512]{1,0:T(8,128)} collective-permute-done((f32[2048,512]{1,0:T(8,128)}, f32[2048,512]{1,0:T(8,128)}, u32[]{:S(2)}, u32[]{:S(2)}) %collective-permute-start.2) | collective-permute-done | bytes 4194336 | tf_op jit(solution)/shard_map/ppermute | solution.py:10
  323.3 2.7 dynamic-slice_select_fusion.1
  326.0 0.0 all-gather.5.cloned.1.call-update
  326.0 2.7 fusion.10
  328.7 31.9 %all-gather.5.cloned.1.call-done = f32[512,2048]{1,0:T(8,128)} async-done(((f32[512,512]{1,0:T(8,128)}), f32[512,2048]{1,0:T(8,128)}) %all-gather.5.cloned.1.call-update) | async-done | bytes 4194320 | tf_op jit(solution)/shard_map/all_gather | solution.py:67
  360.6 2.5 reduce_max.38
  363.1 5.8 %add_add_fusion = f32[512,512]{1,0:T(8,128)} fusion(f32[512]{0:T(512)S(1)} %fusion.10, f32[512]{0:T(512)S(1)} %reduce_max.38, f32[2048,512]{1,0:T(8,128)} %collective-permute-done.2, f32[2048,512]{1,0:T(8,128)} %maximum_select_fusion, pred[]{:T(512)S(6)} %eq.38, f32[512,2048]{1,0:T(8,128)} %all-gather.5.cloned.1.call-done), kind=kOutput, calls=%fused_computation.23 | convolution fusion | flops 1079508992 | bytes 13635585 | tf_op jit(solution)/shard_map/dot_general | solution.py:29
  (2 shorter events, 0.0 us)
Async XLA Ops:
  6.5 163.5 %all-gather.3.cloned.1.call-start = ((), (), s32[]{:S(2)}) async-start(), calls=%async_computation | async-start | bytes 10485760 | tf_op jit(solution)/shard_map/all_gather | solution.py:51
  12.2 93.8 %collective-permute-start = (f32[2048,512]{1,0:T(8,128)}, f32[2048,512]{1,0:T(8,128)}, u32[]{:S(2)}, u32[]{:S(2)}) collective-permute-start(f32[2048,512]{1,0:T(8,128)} %fusion.3), channel_id=1, source_target_pairs={{0,4},{4,0},{8,12},{12,8},{16,20},{20,16},{24,28},{28,24},{1,5},{5... | collective-permute-start | bytes 12582920 | tf_op jit(solution)/shard_map/ppermute | solution.py:10
  110.1 250.6 %all-gather.5.cloned.1.call-start = ((), (), s32[]{:S(2)}) async-start(), calls=%async_computation.1 | async-start | bytes 5242880 | tf_op jit(solution)/shard_map/all_gather | solution.py:67
  180.3 47.9 %collective-permute-start.1 = (f32[1024,512]{1,0:T(8,128)S(1)}, f32[1024,512]{1,0:T(8,128)S(1)}, u32[]{:S(2)}, u32[]{:S(2)}) collective-permute-start(f32[1024,512]{1,0:T(8,128)S(1)} %log_add_fusion), channel_id=1, source_target_pairs={{0,4},{4,0},{8,12},{12,8},{16,20},{20,16},{24,28},{28,24},{1,5},{5... | collective-permute-start | bytes 6291464 | tf_op jit(solution)/shard_map/ppermute | solution.py:10
  231.0 92.2 %collective-permute-start.2 = (f32[2048,512]{1,0:T(8,128)}, f32[2048,512]{1,0:T(8,128)}, u32[]{:S(2)}, u32[]{:S(2)}) collective-permute-start(f32[2048,512]{1,0:T(8,128)} %maximum_select_fusion), channel_id=1, source_target_pairs={{0,8},{4,12},{8,0},{12,4},{16,24},{20,28},{24,16},{28,20},{1,9},{5... | collective-permute-start | bytes 12582920 | tf_op jit(solution)/shard_map/ppermute | solution.py:10
Sparse Core Ops, SparseCore 0:
  110.2 59.7 all-gather.2
  326.1 34.4 all-gather.4
where the time goes:
time: 376 us
  waiting for transfers between devices  317 us (84%)
  other arithmetic  21.3 us (6%)
  matrix products  17.2 us (5%)
  between operations  14.1 us (4%)
  starting transfers between devices  6 us (2%)
    ppermute x3, waiting for transfers between devices, from_partner(): lax.ppermute(shard, axis, [(i, i ^ 1 << apart) for i in range(lax.axis_si...  228 us
    all_gather x1, waiting for transfers between devices, on_device(): left_full = lax.all_gather(left_slab, 'state', axis=1, tiled=True)  57.2 us
    all_gather x1, waiting for transfers between devices, on_device(): quad_left = lax.all_gather(quad_slab, 'state', axis=1, tiled=True)  31.9 us
    dot_general x2, matrix products, combine(): summed = jnp.dot(lead, trail, preferred_element_type=jnp.float32)  12.3 us
  transfers between devices with their start and end apart: 5, of which 5 were waited for; matrix products, arithmetic and copies ran while one was open for 1% of the time, Pallas kernels for 0%

commit v1 on v0

--- a/solution.py
+++ b/solution.py
@@ -2,8 +2,29 @@
 import jax.numpy as jnp
 from jax import lax
 from jax.sharding import PartitionSpec as P
+from jax.lax import axis_index, axis_size, ppermute
 
 BLOCK = 128
+
+
+def points_get(v0, axis_k):
+    wide_out = list(v0.shape[1:])
+    wide_out[axis_k] *= v0.shape[0]
+    return jnp.moveaxis(v0, 0, axis_k).reshape(wide_out)
+
+
+def local_data_wrap(chunk, shard_axis):
+    n_peers_all = axis_size(shard_axis)
+    a_now = chunk[None]
+    for rr in range(n_peers_all.bit_length() - 1):
+        arr_now = 1 << rr
+        placed = ppermute(
+            a_now, shard_axis, list(map(lambda pp: (pp, pp ^ arr_now), range(n_peers_all)))
+        )
+        taken_in = jnp.stack([a_now, placed], 0)
+        reply = axis_index(shard_axis) >> rr & 1
+        a_now = jnp.where(reply == 0, taken_in, taken_in[::-1]).reshape(-1, *chunk.shape)
+    return a_now
 
 
 def from_partner(shard, axis, apart):
@@ -48,7 +69,7 @@
     row_start = half_index * (states // 2)
     row_count = states // 2
     left_slab = lax.dynamic_slice_in_dim(first_op, row_start, row_count, 0)
-    left_full = lax.all_gather(left_slab, "state", axis=1, tiled=True)
+    left_full = points_get(local_data_wrap(left_slab, "state"), 1)
     pair_op = combine(left_full, second_op)
     other_half = from_partner(pair_op, "tm", 0)
     own_pair = jnp.where(

time: 376 us -> 421 us (1.12)
  waiting for transfers between devices: 317 us -> 353 us
  other arithmetic: 21.3 us -> 29.8 us
    ppermute x0 -> x2, waiting for transfers between devices: none -> 92.9 us  [local_data_wrap(): ppermute(a_now, shard_axis, list(map(lambda pp: (pp, pp ^ arr_now), range...]
    all_gather x1 -> x0, waiting for transfers between devices: 57.2 us -> none  [on_device(): left_full = lax.all_gather(left_slab, 'state', axis=1, tiled=True)]
    another operation x0 -> x4, other arithmetic: none -> 13.8 us  [local_data_wrap(): taken_in = jnp.stack([a_now, placed], 0)]
  transfers between devices with their start and end apart: 5 -> 6, of which waited for: 5 -> 6; matrix products, arithmetic and copies ran while one was open for 1% -> 1% of each run, Pallas kernels for 0% -> 0%
where the time goes in v1:
time: 421 us
  waiting for transfers between devices  353 us (84%)
  other arithmetic  29.8 us (7%)
  matrix products  14.1 us (3%)
  between operations  14.1 us (3%)
  starting transfers between devices  6.57 us (2%)
    ppermute x3, waiting for transfers between devices, from_partner(): lax.ppermute(shard, axis, [(i, i ^ 1 << apart) for i in range(lax.axis_si...  227 us
    ppermute x2, waiting for transfers between devices, local_data_wrap(): ppermute(a_now, shard_axis, list(map(lambda pp: (pp, pp ^ arr_now), range...  92.9 us
    all_gather x1, waiting for transfers between devices, on_device(): quad_left = lax.all_gather(quad_slab, 'state', axis=1, tiled=True)  32.5 us
    another operation x4, other arithmetic, local_data_wrap(): taken_in = jnp.stack([a_now, placed], 0)  13.8 us
    dot_general x2, matrix products, combine(): summed = jnp.dot(lead, trail, preferred_element_type=jnp.float32)  10.8 us
  transfers between devices with their start and end apart: 6, of which 6 were waited for; matrix products, arithmetic and copies ran while one was open for 1% of the time, Pallas kernels for 0%

profile of v1, /device:TPU:0, one launch (start us, length us, event | category | flops | bytes accessed | tf_op | source)
XLA Modules:
  0.0 421.0 jit_solution(12038492962052474470)
XLA Ops:
  6.5 0.0 copy-start.3
  6.5 0.0 copy-start.2
  6.5 0.0 all-gather.2.cloned.1.call-start
  7.2 2.9 copy.5
  10.2 0.0 copy-done.3
  10.2 0.0 copy-done.2
  10.2 3.4 fusion.4
  13.5 2.9 collective-permute-start
  16.5 90.9 %collective-permute-done = f32[2048,512]{0,1:T(8,128)} collective-permute-done((f32[2048,512]{0,1:T(8,128)}, f32[2048,512]{0,1:T(8,128)}, u32[]{:S(2)}, u32[]{:S(2)}) %collective-permute-start) | collective-permute-done | bytes 4194336 | tf_op jit(solution)/shard_map/ppermute | solution.py:31
  107.4 4.2 fusion.17
  111.5 0.0 collective-permute-start.1
  111.5 4.5 %collective-permute-done.1 = f32[1,1024,512]{1,2,0:T(8,128)} collective-permute-done((f32[1,1024,512]{1,2,0:T(8,128)}, f32[1,1024,512]{1,2,0:T(8,128)}, u32[]{:S(2)}, u32[]{:S(2)}) %collective-permute-start.1) | collective-permute-done | bytes 2097184 | tf_op jit(solution)/shard_map/ppermute | solution.py:21
  116.0 1.9 pad_maximum_fusion.1
  117.9 4.3 %fusion.6 = (f32[1,2,1024,512]{2,3,1,0:T(8,128)}, f32[2,1024,512]{1,2,0:T(8,128)}) fusion(f32[2,1,1024,512]{2,3,1,0:T(8,128)S(1)} %pad_maximum_fusion.1, pred[]{:T(512)S(6)} %eq.47), kind=kLoop, calls=%fused_computation.16 | loop fusion | flops 1048576 | bytes 12582913 | tf_op jit(solution)/shard_map/stack;reshape | solution.py:24
  122.2 1.8 collective-permute-start.2
  124.0 0.0 copy-start.1
  124.0 2.8 fusion.12
  126.8 88.4 %collective-permute-done.2 = f32[2,1024,512]{1,2,0:T(8,128)} collective-permute-done((f32[2,1024,512]{1,2,0:T(8,128)}, f32[2,1024,512]{1,2,0:T(8,128)}, u32[]{:S(2)}, u32[]{:S(2)}) %collective-permute-start.2) | collective-permute-done | bytes 4194336 | tf_op jit(solution)/shard_map/ppermute | solution.py:21
  215.2 0.0 copy-done.1
  215.2 3.4 pad_maximum_fusion
  218.6 1.2 fusion.30
  219.8 0.0 copy-start
  219.8 1.4 fusion.1
  221.2 0.8 copy-done
  222.0 4.8 %log_add_fusion = f32[1024,512]{0,1:T(8,128)S(1)} fusion(bf16[1024,2048]{0,1:T(8,128)(2,1)S(1)} %fusion.1, f32[512]{0:T(512)S(1)} %fusion.12, f32[2048,512]{0,1:T(8,128)} %collective-permute-done, f32[2048,512]{0,1:T(8,128)S(1)} %copy-done, pred[]{:T(512)S(6)} %eq.45, f32[1024]{0:T(1024)S(1)} %get-tuple-element.5), kind=kOutput, calls=%fused_computation.22 | convolution fusion | flops 2151677952 | bytes 14686209 | tf_op jit(solution)/shard_map/dot_general | solution.py:50
  226.8 0.1 collective-permute-start.3
  226.9 46.9 %collective-permute-done.3 = f32[1024,512]{0,1:T(8,128)S(1)} collective-permute-done((f32[1024,512]{0,1:T(8,128)S(1)}, f32[1024,512]{0,1:T(8,128)S(1)}, u32[]{:S(2)}, u32[]{:S(2)}) %collective-permute-start.3) | collective-permute-done | bytes 2097184 | tf_op jit(solution)/shard_map/ppermute | solution.py:31
  273.7 2.7 maximum_select_fusion
  276.5 1.8 collective-permute-start.4
  278.2 89.4 %collective-permute-done.4 = f32[2048,512]{0,1:T(8,128)} collective-permute-done((f32[2048,512]{0,1:T(8,128)}, f32[2048,512]{0,1:T(8,128)}, u32[]{:S(2)}, u32[]{:S(2)}) %collective-permute-start.4) | collective-permute-done | bytes 4194336 | tf_op jit(solution)/shard_map/ppermute | solution.py:31
  367.7 2.7 dynamic-slice_select_fusion.1
  370.4 0.0 all-gather.2.cloned.1.call-update
  370.4 2.6 fusion.13
  373.1 32.5 %all-gather.2.cloned.1.call-done = f32[512,2048]{0,1:T(8,128)} async-done(((f32[512,512]{0,1:T(8,128)}), f32[512,2048]{0,1:T(8,128)}) %all-gather.2.cloned.1.call-update) | async-done | bytes 4194320 | tf_op jit(solution)/shard_map/all_gather | solution.py:88
  405.6 2.5 reduce_max.38
  408.1 6.0 %add_add_fusion = f32[512,512]{1,0:T(8,128)} fusion(f32[512]{0:T(512)S(1)} %fusion.13, f32[512]{0:T(512)S(1)} %reduce_max.38, f32[2048,512]{0,1:T(8,128)} %collective-permute-done.4, f32[2048,512]{0,1:T(8,128)} %maximum_select_fusion, pred[]{:T(512)S(6)} %eq.44, f32[512,2048]{0,1:T(8,128)} %all-gather.2.cloned.1.call-done), kind=kOutput, calls=%fused_computation.30 | convolution fusion | flops 1079508992 | bytes 13635585 | tf_op jit(solution)/shard_map/dot_general | solution.py:50
  (2 shorter events, 0.0 us)
Async XLA Ops:
  6.5 3.6 copy-start.3
  6.5 3.6 copy-start.2
  6.5 399.0 %all-gather.2.cloned.1.call-start = ((), (), s32[]{:S(2)}) async-start(), calls=%async_computation | async-start | bytes 5242880 | tf_op jit(solution)/shard_map/all_gather | solution.py:88
  13.5 93.8 %collective-permute-start = (f32[2048,512]{0,1:T(8,128)}, f32[2048,512]{0,1:T(8,128)}, u32[]{:S(2)}, u32[]{:S(2)}) collective-permute-start(f32[2048,512]{0,1:T(8,128)} %fusion.4), channel_id=1, source_target_pairs={{0,4},{4,0},{8,12},{12,8},{16,20},{20,16},{24,28},{28,24},{1,5},{5... | collective-permute-start | bytes 12582920 | tf_op jit(solution)/shard_map/ppermute | solution.py:31
  111.5 4.5 %collective-permute-start.1 = (f32[1,1024,512]{1,2,0:T(8,128)}, f32[1,1024,512]{1,2,0:T(8,128)}, u32[]{:S(2)}, u32[]{:S(2)}) collective-permute-start(f32[1,1024,512]{1,2,0:T(8,128)} %get-tuple-element.8), channel_id=1, source_target_pairs={{0,1},{1,0},{2,3},{3,2},{4,5},{5,4},{6,7},{7,6},{8,9},{9,8},{10,11... | collective-permute-start | bytes 6291464 | tf_op jit(solution)/shard_map/ppermute | solution.py:21
  122.2 93.0 %collective-permute-start.2 = (f32[2,1024,512]{1,2,0:T(8,128)}, f32[2,1024,512]{1,2,0:T(8,128)}, u32[]{:S(2)}, u32[]{:S(2)}) collective-permute-start(f32[2,1024,512]{1,2,0:T(8,128)} %get-tuple-element.10), channel_id=1, source_target_pairs={{0,2},{1,3},{2,0},{3,1},{4,6},{5,7},{6,4},{7,5},{8,10},{9,11},{10,... | collective-permute-start | bytes 12582920 | tf_op jit(solution)/shard_map/ppermute | solution.py:21
  124.0 91.2 %copy-start.1 = (f32[1,2,1024,512]{2,3,1,0:T(8,128)S(1)}, f32[1,2,1024,512]{2,3,1,0:T(8,128)}, u32[]{:S(2)}) copy-start(f32[1,2,1024,512]{2,3,1,0:T(8,128)} %get-tuple-element.9) | copy-start | bytes 12582916
  219.8 2.2 copy-start
  226.8 46.9 %collective-permute-start.3 = (f32[1024,512]{0,1:T(8,128)S(1)}, f32[1024,512]{0,1:T(8,128)S(1)}, u32[]{:S(2)}, u32[]{:S(2)}) collective-permute-start(f32[1024,512]{0,1:T(8,128)S(1)} %log_add_fusion), channel_id=1, source_target_pairs={{0,4},{4,0},{8,12},{12,8},{16,20},{20,16},{24,28},{28,24},{1,5},{5... | collective-permute-start | bytes 6291464 | tf_op jit(solution)/shard_map/ppermute | solution.py:31
  276.5 91.2 %collective-permute-start.4 = (f32[2048,512]{0,1:T(8,128)}, f32[2048,512]{0,1:T(8,128)}, u32[]{:S(2)}, u32[]{:S(2)}) collective-permute-start(f32[2048,512]{0,1:T(8,128)} %maximum_select_fusion), channel_id=1, source_target_pairs={{0,8},{4,12},{8,0},{12,4},{16,24},{20,28},{24,16},{28,20},{1,9},{5... | collective-permute-start | bytes 12582920 | tf_op jit(solution)/shard_map/ppermute | solution.py:31
Sparse Core Ops, SparseCore 0:
  370.5 34.9 all-gather.1
